TPU v7x, 512 devices: a whole 4x4x16 slice. The times are simulated.
512 devices in a mesh: dp: 128 (over z, y, core), mp: 4 (over x).
Axes of the slice: x: 4, y: 4, z: 16, core: 2. Of those that a mesh axis runs over, the one named last changes fastest.
Arguments:
- item_table: bfloat16 [262144, 256], P('dp'), may hold values from -6 to 6
- history_owner: int32 [32768, 1], P(('dp', 'mp')), may hold values from 0 to 127; in each aligned block of 64 rows (0 to 63, 64 to 127, ...) at most 4 rows name the same one
- history_row: int32 [32768], P(('dp', 'mp')), may hold values from 0 to 2047
- w_in: bfloat16 [256, 512], replicated, may hold values from -0.375 to 0.375
- conv_a: bfloat16 [4, 3, 512, 512], P(None, None, None, 'mp'), may hold values from -0.15625 to 0.15625
- conv_b: bfloat16 [4, 3, 512, 512], P(None, None, 'mp'), may hold values from -0.15625 to 0.15625
- gains: float32 [4, 512], replicated, may hold values from 0.5 to 1.5
- w_out: bfloat16 [512, 256], replicated, may hold values from -0.25 to 0.25
- cand_row: int32 [128, 128, 8], P('dp'), may hold values from 0 to 2047
- cand_count: int32 [128, 128], P('dp'), may hold values from 1 to 8, 512 in all within a row
- pos_owner: int32 [128], P('dp'), may hold values from 0 to 127
Outputs:
- scores: float32 [128, 128, 8], P('dp')
- user_loss: float32 [128], P('dp')
Inputs may be any that keep to these rules, and one draw needn't show every extreme that they name: `history_owner`: within each aligned block of 64 events no owner appears more than 4 times, and some owner appears exactly 4 times. `cand_count`: each user's counts sum to 512; the largest of them is 8.
All inputs are finite; a program needn't handle non-finite values.
Results may differ from a plain program's by a relative error of at most 0.025.
Values may be sent and summed in bfloat16 or wider, within the bound.
No kernel may reach another device: no remote copies, remote signals or barrier semaphores. Data moves between devices by JAX's collectives and lax.ppermute only.
A program may use at most 64 MiB of HBM per device.

v0:
```python
import jax
import jax.numpy as jnp
from jax import lax
from jax.sharding import PartitionSpec as P

C = 512
BLOCKS = 4
LEN = 256


def shift_rows(values, offset):
    padded = jnp.pad(values, ((0, 0), (offset, 0), (0, 0)))
    return padded[:, : values.shape[1], :]


def causal_taps(values, dilation):
    return jnp.concatenate(
        [values, shift_rows(values, dilation), shift_rows(values, 2 * dilation)], axis=-1
    )


def lookup(item_table, owner_ids, row_ids, fetch_len, capacity, dp_count):
    groups = owner_ids.shape[0] // fetch_len
    owner_grid = owner_ids.reshape(groups, fetch_len)
    onehot = (
        owner_grid[:, :, None] == jnp.arange(dp_count, dtype=jnp.int32)[None, None, :]
    ).astype(jnp.int32)
    before = jnp.cumsum(onehot, axis=1) - onehot
    slot_within = jnp.sum(before * onehot, axis=2)
    slot_ids = (slot_within + jnp.arange(groups, dtype=jnp.int32)[:, None] * capacity).reshape(-1)
    flat_owner = owner_grid.reshape(-1)
    requests = (
        jnp.zeros((groups * capacity, dp_count), jnp.int32).at[slot_ids, flat_owner].set(row_ids)
    )
    picked = item_table[lax.all_to_all(requests, "dp", split_axis=1, concat_axis=1, tiled=True)]
    arrived = lax.all_to_all(picked, "dp", split_axis=1, concat_axis=1, tiled=True)
    return arrived[slot_ids, flat_owner]


def per_device(
    item_table,
    history_owner,
    history_row,
    w_in,
    conv_a,
    conv_b,
    gains,
    w_out,
    cand_row,
    cand_count,
    pos_owner,
):
    dp_count = lax.axis_size("dp")
    mp_count = lax.axis_size("mp")
    fetch_len = history_row.shape[0]
    capacity = max(4, 2 * fetch_len // dp_count)
    owner_ids = history_owner[:, 0]
    embedded = lookup(item_table, owner_ids, history_row, fetch_len, capacity, dp_count)
    embedded = lax.all_gather(embedded, "mp", axis=0, tiled=True)
    user_count = cand_row.shape[0]
    hidden = jnp.dot(embedded, w_in, preferred_element_type=jnp.float32).astype(jnp.bfloat16)
    quarter = C // mp_count
    for block_idx in range(BLOCKS):
        dilation = 1 if block_idx % 2 == 0 else 4
        taps_a = causal_taps(hidden.reshape(user_count, LEN, C), dilation).reshape(-1, 3 * C)
        rectified = jax.nn.relu(
            jnp.dot(
                taps_a,
                conv_a[block_idx].reshape(3 * C, quarter),
                preferred_element_type=jnp.float32,
            )
        ).astype(jnp.bfloat16)
        taps_b = causal_taps(rectified.reshape(user_count, LEN, quarter), 2 * dilation).reshape(
            -1, 3 * quarter
        )
        partial_value = jnp.dot(
            taps_b, conv_b[block_idx].reshape(3 * quarter, C), preferred_element_type=jnp.float32
        )
        gain_row = gains[block_idx]
        branch = lax.psum(partial_value.astype(jnp.bfloat16), "mp").astype(jnp.float32)
        summed = hidden.astype(jnp.float32) + branch
        row_mean = jnp.mean(summed, axis=1, keepdims=True)
        row_msq = jnp.mean(summed * summed, axis=1, keepdims=True)
        row_var = row_msq - row_mean * row_mean
        hidden = ((summed - row_mean) * lax.rsqrt(row_var + 1e-05) * gain_row).astype(jnp.bfloat16)
    last_rows = hidden.reshape(user_count, LEN, C)[:, LEN - 1, :]
    user_vec = jnp.dot(last_rows, w_out, preferred_element_type=jnp.float32).astype(jnp.bfloat16)
    cand_rows = lax.all_to_all(
        item_table[lax.all_to_all(cand_row, "dp", split_axis=1, concat_axis=1, tiled=True)],
        "dp",
        split_axis=1,
        concat_axis=1,
        tiled=True,
    )
    raw_scores = 0.25 * jnp.einsum(
        "ue,unce->unc", user_vec, cand_rows, preferred_element_type=jnp.float32
    )
    valid_slot = (
        jnp.arange(raw_scores.shape[2], dtype=jnp.int32)[None, None, :] < cand_count[:, :, None]
    )
    scores = jnp.where(valid_slot, raw_scores, 0.0)
    exp_total = jnp.sum(jnp.where(valid_slot, jnp.exp(raw_scores), 0.0), axis=(1, 2))
    positive = jnp.take_along_axis(raw_scores[:, :, 0], pos_owner[:, None], axis=1)[:, 0]
    user_loss = jnp.log(exp_total) - positive
    return (scores, user_loss)


def solution(mesh):
    return jax.shard_map(
        per_device,
        mesh=mesh,
        in_specs=(
            P("dp", None),
            P(("dp", "mp"), None),
            P(("dp", "mp")),
            P(),
            P(None, None, None, "mp"),
            P(None, None, "mp", None),
            P(),
            P(),
            P("dp", None, None),
            P("dp", None),
            P("dp"),
        ),
        out_specs=(P("dp", None, None), P("dp")),
        check_vma=False,
    )
```

profile of v0, /device:TPU:8, one launch (start us, length us, event | category | flops | bytes accessed | tf_op | source)
XLA Modules:
  0.0 346.0 jit_solution(17920219697878644076)
XLA Ops:
  9.6 5.7 %scatter_fusion = s32[4,128]{1,0:T(4,128)S(1)} fusion(s32[4,128]{1,0:T(4,128)S(1)} %broadcast.205, s32[64]{0:T(128)S(1)} %get-tuple-element.21, s32[64]{0:T(128)} %param.13), kind=kCustom, calls=%fused_computation.3 | custom fusion | bytes 1280 | tf_op jit(solution)/shard_map/scatter | solution.py:33
  15.5 33.3 %all_to_all.24 = s32[4,128,1]{0,2,1:T(1,128)S(1)} all-to-all(s32[4,128,1]{0,2,1:T(1,128)S(1)} %copy.19), channel_id=1, replica_groups=mesh['dp'=128,'mp'=4] {'dp'}, dimensions={1} | all-to-all | bytes 4096 | tf_op jit(solution)/shard_map/all_to_all | solution.py:35
  48.9 2.0 gather_fusion
  50.9 0.9 copy.21
  51.8 6.6 %all-to-all-start.1 = ((bf16[4,128,256]{2,0,1:T(4,128)(2,1)}), bf16[4,128,256]{2,0,1:T(4,128)(2,1)S(1)}, u32[]{:S(2)}, u32[]{:S(2)}) async-start(bf16[4,128,256]{2,0,1:T(4,128)(2,1)} %copy.21), calls=%async_computation.1 | async-start | bytes 524288 | tf_op jit(solution)/shard_map/all_to_all | solution.py:36
  58.5 1.1 fusion.62
  60.3 1.0 fusion.63
  61.3 18.6 %all-to-all-done.1 = bf16[4,128,256]{2,0,1:T(4,128)(2,1)S(1)} async-done(((bf16[4,128,256]{2,0,1:T(4,128)(2,1)}), bf16[4,128,256]{2,0,1:T(4,128)(2,1)S(1)}, u32[]{:S(2)}, u32[]{:S(2)}) %all-to-all-start.1) | async-done | bytes 262176 | tf_op jit(solution)/shard_map/all_to_all | solution.py:36
  80.8 12.3 %all_gather.3 = bf16[256,256]{1,0:T(8,128)(2,1)S(1)} all-gather(bf16[64,256]{1,0:T(8,128)(2,1)S(1)} %gather_fusion.1), channel_id=1, replica_groups=mesh['dp'=128,'mp'=4] {'mp'}, dimensions={0}, use_global_device_ids=true | all-gather | bytes 163840 | tf_op jit(solution)/shard_map/all_gather | solution.py:59
  93.5 1.4 fusion.7
  95.0 1.0 convolution_convert_fusion.3
  96.1 49.1 %all-reduce.21.cloned.1.call-done = bf16[256,512]{1,0:T(8,128)(2,1)} async-done(((bf16[256,512]{1,0:T(8,128)(2,1)}), bf16[256,512]{1,0:T(8,128)(2,1)}) %all-reduce.21.cloned.1.call-update) | async-done | bytes 262160 | tf_op jit(solution)/shard_map/psum | solution.py:80
  145.2 1.1 fusion.26
  146.4 1.1 multiply_convert_fusion.3
  148.0 1.0 convolution_convert_fusion.2
  149.7 16.5 %all-to-all-start.2 = ((s32[1,128,8]{2,0,1:T(1,128)}), s32[1,128,8]{2,0,1:T(1,128)S(1)}, u32[]{:S(2)}, u32[]{:S(2)}) async-start(s32[1,128,8]{2,0,1:T(1,128)} %copy.23), calls=%async_computation.2 | async-start | bytes 131072 | tf_op jit(solution)/shard_map/all_to_all | solution.py:89
  166.3 40.6 %all-reduce.23.cloned.1.call-done = bf16[256,512]{1,0:T(8,128)(2,1)} async-done(((bf16[256,512]{1,0:T(8,128)(2,1)}), bf16[256,512]{1,0:T(8,128)(2,1)}) %all-reduce.23.cloned.1.call-update) | async-done | bytes 262160 | tf_op jit(solution)/shard_map/psum | solution.py:80
  206.9 1.1 fusion.27
  208.1 1.1 multiply_convert_fusion.2
  209.3 1.4 fusion.5
  210.8 1.0 convolution_convert_fusion.1
  212.1 5.0 %gather_fusion.2 = bf16[1024,256]{1,0:T(8,128)(2,1)} fusion(bf16[2048,256]{1,0:T(8,128)(2,1)S(1)} %copy-done, s32[1024]{0:T(1024)S(1)} %broadcast_clamp_fusion), kind=kCustom, calls=%fused_computation.2 | custom fusion | bytes 1052672 | tf_op jit(solution)/shard_map/gather | solution.py:89
  217.1 16.5 %all-to-all-start.3 = ((bf16[1,128,8,256]{3,2,0,1:T(8,128)(2,1)}), bf16[1,128,8,256]{3,2,0,1:T(8,128)(2,1)S(1)}, u32[]{:S(2)}, u32[]{:S(2)}) async-start(bf16[1,128,8,256]{3,2,0,1:T(8,128)(2,1)} %bitcast.39), calls=%async_computation.3 | async-start | bytes 1048576 | tf_op jit(solution)/shard_map/all_to_all | solution.py:88
  233.7 36.1 %all-reduce.25.cloned.1.call-done = bf16[256,512]{1,0:T(8,128)(2,1)} async-done(((bf16[256,512]{1,0:T(8,128)(2,1)}), bf16[256,512]{1,0:T(8,128)(2,1)}) %all-reduce.25.cloned.1.call-update) | async-done | bytes 262160 | tf_op jit(solution)/shard_map/psum | solution.py:80
  269.8 1.1 fusion.28
  270.9 1.1 multiply_convert_fusion.1
  272.5 1.0 convolution_convert_fusion
  274.2 57.3 %all-reduce.27.cloned.1.call-done = bf16[256,512]{1,0:T(8,128)(2,1)} async-done(((bf16[256,512]{1,0:T(8,128)(2,1)}), bf16[256,512]{1,0:T(8,128)(2,1)}) %all-reduce.27.cloned.1.call-update) | async-done | bytes 262160 | tf_op jit(solution)/shard_map/psum | solution.py:80
  331.5 1.1 fusion.29
  332.6 1.1 fusion.30
  333.9 1.2 fusion.24
  335.2 1.2 select_reduce_fusion.1
  (69 shorter events, 7.9 us)
Async XLA Ops:
  7.2 41.7 %copy-start = (bf16[2048,256]{1,0:T(8,128)(2,1)S(1)}, bf16[2048,256]{1,0:T(8,128)(2,1)}, u32[]{:S(2)}) copy-start(bf16[2048,256]{1,0:T(8,128)(2,1)} %param.11) | copy-start | bytes 3145732
  48.9 9.6 %copy-start.1 = (bf16[4,3,512,128]{3,2,1,0:T(8,128)(2,1)S(1)}, bf16[4,3,512,128]{3,2,1,0:T(8,128)(2,1)}, u32[]{:S(2)}) copy-start(bf16[4,3,512,128]{3,2,1,0:T(8,128)(2,1)} %param.15) | copy-start | bytes 4718596
  51.8 28.2 %all-to-all-start.1 = ((bf16[4,128,256]{2,0,1:T(4,128)(2,1)}), bf16[4,128,256]{2,0,1:T(4,128)(2,1)S(1)}, u32[]{:S(2)}, u32[]{:S(2)}) async-start(bf16[4,128,256]{2,0,1:T(4,128)(2,1)} %copy.21), calls=%async_computation.1 | async-start | bytes 524288 | tf_op jit(solution)/shard_map/all_to_all | solution.py:36
  58.5 86.8 %all-reduce.21.cloned.1.call-start = ((), (), s32[]{:S(2)}) async-start(), calls=%async_computation.4 | async-start | bytes 524288 | tf_op jit(solution)/shard_map/psum | solution.py:80
  58.5 1.8 copy-start.2
  60.3 32.8 %copy-start.6 = (bf16[256,512]{1,0:T(8,128)(2,1)S(1)}, bf16[256,512]{1,0:T(8,128)(2,1)}, u32[]{:S(2)}) copy-start(bf16[256,512]{1,0:T(8,128)(2,1)} %param.14) | copy-start | bytes 786436
  93.5 1.5 copy-start.5
  93.5 2.6 copy-start.8
  95.0 52.6 %copy-start.4 = (bf16[1,3,512,128]{3,2,1,0:T(8,128)(2,1)S(1)}, bf16[1,3,512,128]{3,2,1,0:T(8,128)(2,1)}, u32[]{:S(2)}) copy-start(bf16[1,3,512,128]{3,2,1,0:T(8,128)(2,1)} %get-tuple-element.24) | copy-start | bytes 1179652
  96.0 110.9 %all-reduce.23.cloned.1.call-start = ((), (), s32[]{:S(2)}) async-start(), calls=%async_computation.5 | async-start | bytes 524288 | tf_op jit(solution)/shard_map/psum | solution.py:80
  147.6 1.4 copy-start.9
  149.7 62.1 %all-to-all-start.2 = ((s32[1,128,8]{2,0,1:T(1,128)}), s32[1,128,8]{2,0,1:T(1,128)S(1)}, u32[]{:S(2)}, u32[]{:S(2)}) async-start(s32[1,128,8]{2,0,1:T(1,128)} %copy.23), calls=%async_computation.2 | async-start | bytes 131072 | tf_op jit(solution)/shard_map/all_to_all | solution.py:89
  166.2 103.5 %all-reduce.25.cloned.1.call-start = ((), (), s32[]{:S(2)}) async-start(), calls=%async_computation.6 | async-start | bytes 524288 | tf_op jit(solution)/shard_map/psum | solution.py:80
  209.3 1.5 copy-start.3
  217.1 116.8 %all-to-all-start.3 = ((bf16[1,128,8,256]{3,2,0,1:T(8,128)(2,1)}), bf16[1,128,8,256]{3,2,0,1:T(8,128)(2,1)S(1)}, u32[]{:S(2)}, u32[]{:S(2)}) async-start(bf16[1,128,8,256]{3,2,0,1:T(8,128)(2,1)} %bitcast.39), calls=%async_computation.3 | async-start | bytes 1048576 | tf_op jit(solution)/shard_map/all_to_all | solution.py:88
  233.6 97.9 %all-reduce.27.cloned.1.call-start = ((), (), s32[]{:S(2)}) async-start(), calls=%async_computation.7 | async-start | bytes 524288 | tf_op jit(solution)/shard_map/psum | solution.py:80
  272.5 61.3 %copy-start.7 = (bf16[512,256]{1,0:T(8,128)(2,1)S(1)}, bf16[512,256]{1,0:T(8,128)(2,1)}, u32[]{:S(2)}) copy-start(bf16[512,256]{1,0:T(8,128)(2,1)} %param.18) | copy-start | bytes 786436
  272.5 62.7 %copy-start.10 = (s32[1,128]{1,0:T(1,128)S(1)}, s32[1,128]{1,0:T(1,128)}, u32[]{:S(2)}) copy-start(s32[1,128]{1,0:T(1,128)} %param.20) | copy-start | bytes 1540
Sparse Core Ops, SparseCore 0:
  96.1 49.0 all-reduce.20
  149.1 57.7 all-reduce.22
  211.9 57.7 all-reduce.24
  273.7 57.7 all-reduce.26
where the time goes:
time: 347 us; the launch traced here: 346 us
  waiting for transfers between devices  202 us (58%)
  blocking collectives  45.6 us (13%)
  starting transfers between devices  39.8 us (11%)
  local copies, waits for them, and re-layouts  19.4 us (6%)
  between operations  17.2 us (5%)
  other arithmetic  12.9 us (4%)
  matrix products  9.16 us (3%)
    psum x4, waiting for transfers between devices, per_device(): lax.psum(partial_value.astype(jnp.bfloat16), 'mp').astype(jnp.float32)  183 us
    all_to_all x1, blocking collectives, lookup(): lax.all_to_all(requests, 'dp', split_axis=1, concat_axis=1, tiled=True)  33.3 us
    all_to_all x1, waiting for transfers between devices, lookup(): lax.all_to_all(picked, 'dp', split_axis=1, concat_axis=1, tiled=True)  18.6 us
    all_to_all x1, starting transfers between devices, per_device(): lax.all_to_all(cand_row, 'dp', split_axis=1, concat_axis=1, tiled=True)  16.5 us
    all_to_all x1, starting transfers between devices, per_device(): lax.all_to_all(item_table[lax.all_to_all(cand_row, 'dp', split_axis=1, co...  16.5 us
    all_gather x1, blocking collectives, per_device(): embedded = lax.all_gather(embedded, 'mp', axis=0, tiled=True)  12.3 us
  transfers between devices with their start and end apart: 7, of which 5 were waited for; matrix products, arithmetic and copies ran while one was open for 5% of the time, Pallas kernels for 0%

commit v1 on v0

--- a/solution.py
+++ b/solution.py
@@ -77,7 +77,9 @@
             taps_b, conv_b[block_idx].reshape(3 * quarter, C), preferred_element_type=jnp.float32
         )
         gain_row = gains[block_idx]
-        branch = lax.psum(partial_value.astype(jnp.bfloat16), "mp").astype(jnp.float32)
+        branch = jnp.sum(lax.all_gather(partial_value.astype(jnp.bfloat16), "mp"), axis=0).astype(
+            jnp.float32
+        )
         summed = hidden.astype(jnp.float32) + branch
         row_mean = jnp.mean(summed, axis=1, keepdims=True)
         row_msq = jnp.mean(summed * summed, axis=1, keepdims=True)

time: 347 us -> 264 us (0.76)
  the two profiles are of different devices: /device:TPU:8 before, /device:TPU:33 now
where the time goes in v1:
time: 264 us; the launch traced here: 263 us
  waiting for transfers between devices  119 us (45%)
  starting transfers between devices  44.2 us (17%)
  blocking collectives  43.3 us (16%)
  local copies, waits for them, and re-layouts  20.5 us (8%)
  between operations  17.3 us (7%)
  other arithmetic  11.2 us (4%)
  matrix products  8.09 us (3%)
    all_gather x4, waiting for transfers between devices, per_device(): lax.all_gather(partial_value.astype(jnp.bfloat16), 'mp')  75.6 us
    all_to_all x1, blocking collectives, lookup(): lax.all_to_all(requests, 'dp', split_axis=1, concat_axis=1, tiled=True)  33.5 us
    all_to_all x1, waiting for transfers between devices, per_device(): lax.all_to_all(item_table[lax.all_to_all(cand_row, 'dp', split_axis=1, co...  23.3 us
    all_to_all x1, waiting for transfers between devices, lookup(): lax.all_to_all(picked, 'dp', split_axis=1, concat_axis=1, tiled=True)  19.7 us
    all_to_all x1, starting transfers between devices, per_device(): lax.all_to_all(cand_row, 'dp', split_axis=1, concat_axis=1, tiled=True)  18.8 us
    all_to_all x1, starting transfers between devices, per_device(): lax.all_to_all(item_table[lax.all_to_all(cand_row, 'dp', split_axis=1, co...  18.6 us
    all_gather x1, blocking collectives, per_device(): embedded = lax.all_gather(embedded, 'mp', axis=0, tiled=True)  9.77 us
    all_to_all x1, starting transfers between devices, lookup(): lax.all_to_all(picked, 'dp', split_axis=1, concat_axis=1, tiled=True)  6.4 us
  transfers between devices with their start and end apart: 7, of which 6 were waited for; matrix products, arithmetic and copies ran while one was open for 5% of the time, Pallas kernels for 0%

profile of v1, /device:TPU:33, one launch (start us, length us, event | category | flops | bytes accessed | tf_op | source)
XLA Modules:
  0.0 263.2 jit_solution(16389185279007247481)
XLA Ops:
  7.2 0.8 fusion.48
  8.1 0.8 select_reduce_fusion
  9.6 5.7 %scatter_fusion = s32[4,128]{1,0:T(4,128)S(1)} fusion(s32[4,128]{1,0:T(4,128)S(1)} %broadcast.205, s32[64]{0:T(128)S(1)} %get-tuple-element.21, s32[64]{0:T(128)} %param.13), kind=kCustom, calls=%fused_computation.3 | custom fusion | bytes 1280 | tf_op jit(solution)/shard_map/scatter | solution.py:33
  15.5 33.5 %all_to_all.24 = s32[4,128,1]{0,2,1:T(1,128)S(1)} all-to-all(s32[4,128,1]{0,2,1:T(1,128)S(1)} %copy.19), channel_id=1, replica_groups=mesh['dp'=128,'mp'=4] {'dp'}, dimensions={1} | all-to-all | bytes 4096 | tf_op jit(solution)/shard_map/all_to_all | solution.py:35
  49.1 2.0 gather_fusion
  51.1 0.9 copy.21
  52.0 6.4 %all-to-all-start.1 = ((bf16[4,128,256]{2,0,1:T(4,128)(2,1)}), bf16[4,128,256]{2,0,1:T(4,128)(2,1)S(1)}, u32[]{:S(2)}, u32[]{:S(2)}) async-start(bf16[4,128,256]{2,0,1:T(4,128)(2,1)} %copy.21), calls=%async_computation.1 | async-start | bytes 524288 | tf_op jit(solution)/shard_map/all_to_all | solution.py:36
  58.5 1.0 fusion.62
  59.5 0.8 copy-done.2
  60.3 1.0 fusion.63
  61.3 19.7 %all-to-all-done.1 = bf16[4,128,256]{2,0,1:T(4,128)(2,1)S(1)} async-done(((bf16[4,128,256]{2,0,1:T(4,128)(2,1)}), bf16[4,128,256]{2,0,1:T(4,128)(2,1)S(1)}, u32[]{:S(2)}, u32[]{:S(2)}) %all-to-all-start.1) | async-done | bytes 262176 | tf_op jit(solution)/shard_map/all_to_all | solution.py:36
  81.0 0.8 gather_fusion.1
  81.9 9.8 %all_gather.27 = bf16[256,256]{1,0:T(8,128)(2,1)S(1)} all-gather(bf16[64,256]{1,0:T(8,128)(2,1)S(1)} %gather_fusion.1), channel_id=1, replica_groups=mesh['dp'=128,'mp'=4] {'mp'}, dimensions={0}, use_global_device_ids=true | all-gather | bytes 163840 | tf_op jit(solution)/shard_map/all_gather | solution.py:59
  92.0 1.4 fusion.7
  93.5 1.0 convolution_convert_fusion.3
  94.6 22.8 %all-gather.9.cloned.1.call-done = bf16[1024,512]{1,0:T(8,128)(2,1)} async-done(((bf16[256,512]{1,0:T(8,128)(2,1)}), bf16[1024,512]{1,0:T(8,128)(2,1)}) %all-gather.9.cloned.1.call-update) | async-done | bytes 1048592 | tf_op jit(solution)/shard_map/all_gather | solution.py:80
  117.4 1.5 reduce_sum.142
  120.3 1.0 convolution_convert_fusion.2
  121.4 32.3 %all-gather.11.cloned.1.call-done = bf16[1024,512]{1,0:T(8,128)(2,1)} async-done(((bf16[256,512]{1,0:T(8,128)(2,1)}), bf16[1024,512]{1,0:T(8,128)(2,1)}) %all-gather.11.cloned.1.call-update) | async-done | bytes 1048592 | tf_op jit(solution)/shard_map/all_gather | solution.py:80
  153.7 1.5 reduce_sum.145
  156.5 1.0 convolution_convert_fusion.1
  158.3 18.8 %all-to-all-start.2 = ((s32[1,128,8]{2,0,1:T(1,128)}), s32[1,128,8]{2,0,1:T(1,128)S(1)}, u32[]{:S(2)}, u32[]{:S(2)}) async-start(s32[1,128,8]{2,0,1:T(1,128)} %copy.23), calls=%async_computation.2 | async-start | bytes 131072 | tf_op jit(solution)/shard_map/all_to_all | solution.py:91
  177.3 12.8 %all-gather.13.cloned.1.call-done = bf16[1024,512]{1,0:T(8,128)(2,1)} async-done(((bf16[256,512]{1,0:T(8,128)(2,1)}), bf16[1024,512]{1,0:T(8,128)(2,1)}) %all-gather.13.cloned.1.call-update) | async-done | bytes 1048592 | tf_op jit(solution)/shard_map/all_gather | solution.py:80
  190.1 1.5 reduce_sum.148
  192.4 1.0 convolution_convert_fusion
  193.7 5.0 %gather_fusion.2 = bf16[1024,256]{1,0:T(8,128)(2,1)} fusion(bf16[2048,256]{1,0:T(8,128)(2,1)S(1)} %copy-done, s32[1024]{0:T(1024)S(1)} %broadcast_clamp_fusion), kind=kCustom, calls=%fused_computation.2 | custom fusion | bytes 1052672 | tf_op jit(solution)/shard_map/gather | solution.py:91
  198.7 18.6 %all-to-all-start.3 = ((bf16[1,128,8,256]{3,2,0,1:T(8,128)(2,1)}), bf16[1,128,8,256]{3,2,0,1:T(8,128)(2,1)S(1)}, u32[]{:S(2)}, u32[]{:S(2)}) async-start(bf16[1,128,8,256]{3,2,0,1:T(8,128)(2,1)} %bitcast.43), calls=%async_computation.3 | async-start | bytes 1048576 | tf_op jit(solution)/shard_map/all_to_all | solution.py:90
  218.0 7.7 %all-gather.15.cloned.1.call-done = bf16[1024,512]{1,0:T(8,128)(2,1)} async-done(((bf16[256,512]{1,0:T(8,128)(2,1)}), bf16[1024,512]{1,0:T(8,128)(2,1)}) %all-gather.15.cloned.1.call-update) | async-done | bytes 1048592 | tf_op jit(solution)/shard_map/all_gather | solution.py:80
  225.8 1.5 reduce_sum.151
  227.8 23.3 %all-to-all-done.3 = bf16[1,128,8,256]{3,2,0,1:T(8,128)(2,1)S(1)} async-done(((bf16[1,128,8,256]{3,2,0,1:T(8,128)(2,1)}), bf16[1,128,8,256]{3,2,0,1:T(8,128)(2,1)S(1)}, u32[]{:S(2)}, u32[]{:S(2)}) %all-to-all-start.3) | async-done | bytes 524320 | tf_op jit(solution)/shard_map/all_to_all | solution.py:90
  251.0 1.2 fusion.24
  252.4 1.2 select_reduce_fusion.1
  (75 shorter events, 7.7 us)
Async XLA Ops:
  7.2 42.0 %copy-start = (bf16[2048,256]{1,0:T(8,128)(2,1)S(1)}, bf16[2048,256]{1,0:T(8,128)(2,1)}, u32[]{:S(2)}) copy-start(bf16[2048,256]{1,0:T(8,128)(2,1)} %param.11) | copy-start | bytes 3145732
  49.1 9.3 %copy-start.1 = (bf16[4,3,512,128]{3,2,1,0:T(8,128)(2,1)S(1)}, bf16[4,3,512,128]{3,2,1,0:T(8,128)(2,1)}, u32[]{:S(2)}) copy-start(bf16[4,3,512,128]{3,2,1,0:T(8,128)(2,1)} %param.15) | copy-start | bytes 4718596
  52.0 29.0 %all-to-all-start.1 = ((bf16[4,128,256]{2,0,1:T(4,128)(2,1)}), bf16[4,128,256]{2,0,1:T(4,128)(2,1)S(1)}, u32[]{:S(2)}, u32[]{:S(2)}) async-start(bf16[4,128,256]{2,0,1:T(4,128)(2,1)} %copy.21), calls=%async_computation.1 | async-start | bytes 524288 | tf_op jit(solution)/shard_map/all_to_all | solution.py:36
  58.4 58.9 %all-gather.9.cloned.1.call-start = ((), (), s32[]{:S(2)}) async-start(), calls=%async_computation.4 | async-start | bytes 1310720 | tf_op jit(solution)/shard_map/all_gather | solution.py:80
  58.5 1.8 copy-start.2
  60.3 31.3 %copy-start.7 = (bf16[256,512]{1,0:T(8,128)(2,1)S(1)}, bf16[256,512]{1,0:T(8,128)(2,1)}, u32[]{:S(2)}) copy-start(bf16[256,512]{1,0:T(8,128)(2,1)} %param.14) | copy-start | bytes 786436
  92.0 1.5 copy-start.6
  92.0 2.5 copy-start.9
  94.5 59.2 %all-gather.11.cloned.1.call-start = ((), (), s32[]{:S(2)}) async-start(), calls=%async_computation.5 | async-start | bytes 1310720 | tf_op jit(solution)/shard_map/all_gather | solution.py:80
  118.8 1.0 copy-start.5
  119.3 1.0 copy-start.4
  121.3 68.8 %all-gather.13.cloned.1.call-start = ((), (), s32[]{:S(2)}) async-start(), calls=%async_computation.6 | async-start | bytes 1310720 | tf_op jit(solution)/shard_map/all_gather | solution.py:80
  155.1 1.0 copy-start.3
  156.1 1.5 copy-start.10
  158.3 35.1 %all-to-all-start.2 = ((s32[1,128,8]{2,0,1:T(1,128)}), s32[1,128,8]{2,0,1:T(1,128)S(1)}, u32[]{:S(2)}, u32[]{:S(2)}) async-start(s32[1,128,8]{2,0,1:T(1,128)} %copy.23), calls=%async_computation.2 | async-start | bytes 131072 | tf_op jit(solution)/shard_map/all_to_all | solution.py:91
  177.1 48.6 %all-gather.15.cloned.1.call-start = ((), (), s32[]{:S(2)}) async-start(), calls=%async_computation.7 | async-start | bytes 1310720 | tf_op jit(solution)/shard_map/all_gather | solution.py:80
  198.7 52.3 %all-to-all-start.3 = ((bf16[1,128,8,256]{3,2,0,1:T(8,128)(2,1)}), bf16[1,128,8,256]{3,2,0,1:T(8,128)(2,1)S(1)}, u32[]{:S(2)}, u32[]{:S(2)}) async-start(bf16[1,128,8,256]{3,2,0,1:T(8,128)(2,1)} %bitcast.43), calls=%async_computation.3 | async-start | bytes 1048576 | tf_op jit(solution)/shard_map/all_to_all | solution.py:90
  217.3 10.3 %copy-start.8 = (bf16[512,256]{1,0:T(8,128)(2,1)S(1)}, bf16[512,256]{1,0:T(8,128)(2,1)}, u32[]{:S(2)}) copy-start(bf16[512,256]{1,0:T(8,128)(2,1)} %param.18) | copy-start | bytes 786436
  225.8 26.6 %copy-start.11 = (s32[1,128]{1,0:T(1,128)S(1)}, s32[1,128]{1,0:T(1,128)}, u32[]{:S(2)}) copy-start(s32[1,128]{1,0:T(1,128)} %param.20) | copy-start | bytes 1540
Sparse Core Ops, SparseCore 0:
  94.6 22.7 all-gather.8
  121.4 32.1 all-gather.10
  157.7 32.3 all-gather.12
  193.5 32.1 all-gather.14
